TPU v7x, 128 devices: a whole 4x4x4 slice. The times are simulated.
128 devices in a mesh: rep: 8 (over y_hi, z), fsdp: 16 (over x, y_lo, core).
Axes of the slice: x: 4, y: 4 (y_hi: 2, y_lo: 2; y = y_hi * 2 + y_lo), z: 4, core: 2. Of those that a mesh axis runs over, the one named last changes fastest.
Arguments:
- delta_query: bfloat16 [8, 8192, 4096], P('rep', 'fsdp'), may hold values from -60 to 60
- delta_output: bfloat16 [8, 4096, 8192], P('rep', 'fsdp'), may hold values from -60 to 60
- master_query: float32 [8192, 4096], P('fsdp', 'rep'), may hold values from -6 to 6
- master_output: float32 [4096, 8192], P('fsdp', 'rep'), may hold values from -6 to 6
- moment_query: float32 [8192, 4096], P('fsdp', 'rep'), may hold values from -6 to 6
- moment_output: float32 [4096, 8192], P('fsdp', 'rep'), may hold values from -6 to 6
Outputs:
- weights_query: bfloat16 [8192, 4096], P('fsdp')
- weights_output: bfloat16 [4096, 8192], P('fsdp')
- master_next_query: float32 [8192, 4096], P('fsdp', 'rep')
- master_next_output: float32 [4096, 8192], P('fsdp', 'rep')
- moment_next_query: float32 [8192, 4096], P('fsdp', 'rep')
- moment_next_output: float32 [4096, 8192], P('fsdp', 'rep')
All inputs are finite; a program needn't handle non-finite values.
Results may differ from a plain program's by a relative error of at most 0.006.
Values may be sent and summed in bfloat16 or wider, within the bound.
A program may use at most 128 MiB of HBM per device.

v0:
```python
import functools
import math

import jax
import jax.numpy as jnp
from jax import lax
from jax.sharding import Mesh
from jax.sharding import PartitionSpec as P

D = 8192
HD = 128
HEADS = 32
REP = ("rep_0", "rep_1")
REP_FSDP = ("rep_0", "rep_1", "fsdp_0", "fsdp_1", "fsdp_2")
FSDP = ("fsdp_0", "fsdp_1", "fsdp_2")


def split_up(value, dim, peers):
    before, after = (value.shape[:dim], value.shape[dim + 1 :])
    return jnp.moveaxis(value.reshape(*before, peers, -1, *after), dim, 0)


def cut_rows(length, count):
    unit = 8 if length >= 8 * count else 1
    return [length // unit * k // count * unit for k in range(1, count)]


def laid_out(parts, dim):
    lengths = list(parts.shape[1:])
    lengths[dim] *= parts.shape[0]
    return jnp.moveaxis(parts, 0, dim).reshape(lengths)


def several_exchanges(value, axis, pieces, split_dim, concat_dim):
    parts = split_up(value, split_dim, lax.axis_size(axis))
    widest = max(range(1, max(2, parts.ndim - 1)), key=lambda d: parts.shape[d])
    done = []
    for share in jnp.split(parts, cut_rows(parts.shape[widest], pieces), axis=widest):
        if share.size:
            done.append(lax.all_to_all(share, axis, split_axis=0, concat_axis=0, tiled=True))
    return laid_out(jnp.concatenate(done, axis=widest), concat_dim)


def by_axis(value, axes):
    return functools.reduce(lax.psum, axes, value)


def one_gather(arrays, axis, dims):
    line = jnp.concatenate([a.reshape(-1) for a in arrays])
    lines, at, done = (lax.all_gather(line, axis), 0, [])
    for a, dim in zip(arrays, dims):
        parts = lines[:, at : at + a.size].reshape(-1, *a.shape)
        done.append(laid_out(parts, dim))
        at += a.size
    return tuple(done)


def outer_update(mean, factor, master, moment):
    grad = factor * mean
    moment_next = 0.9 * moment + grad
    master_next = master - 0.7 * (grad + 0.9 * moment_next)
    return (master_next, moment_next)


def on_device(delta_query, delta_output, master_query, master_output, moment_query, moment_output):
    pieces_query, pieces_output = (
        several_exchanges(delta_query, REP, 2, 2, 0),
        several_exchanges(delta_output, REP, 2, 2, 0),
    )
    summed_query = jnp.sum(pieces_query.astype(jnp.float32), axis=0)
    summed_output = jnp.sum(pieces_output.astype(jnp.float32), axis=0)
    replicas = lax.axis_size(REP)
    mean_query = summed_query / replicas
    mean_output = summed_output / replicas
    local_squares = jnp.sum(mean_query * mean_query) + jnp.sum(mean_output * mean_output)
    square_sum = by_axis(local_squares, REP_FSDP)
    limit = 0.25 * math.sqrt(2.0 * D * HEADS * HD)
    factor = jnp.minimum(1.0, limit / jnp.sqrt(square_sum + 1e-06))
    master_next_query, moment_next_query = outer_update(
        mean_query, factor, master_query, moment_query
    )
    master_next_output, moment_next_output = outer_update(
        mean_output, factor, master_output, moment_output
    )
    rounded = (master_next_query.astype(jnp.bfloat16), master_next_output.astype(jnp.bfloat16))
    weights_query, weights_output = one_gather((rounded[0], rounded[1]), REP, (1, 1))
    return (
        weights_query,
        weights_output,
        master_next_query,
        master_next_output,
        moment_next_query,
        moment_next_output,
    )


def solution(mesh):
    split = Mesh(
        mesh.devices.reshape(2, 4, 4, 2, 2), ("rep_0", "rep_1", "fsdp_0", "fsdp_1", "fsdp_2")
    )
    in_specs = (
        P(REP, FSDP, None),
        P(REP, FSDP, None),
        P(FSDP, REP),
        P(FSDP, REP),
        P(FSDP, REP),
        P(FSDP, REP),
    )
    out_specs = (
        P(FSDP, None),
        P(FSDP, None),
        P(FSDP, REP),
        P(FSDP, REP),
        P(FSDP, REP),
        P(FSDP, REP),
    )
    return jax.shard_map(
        on_device, mesh=split, in_specs=in_specs, out_specs=out_specs, check_vma=False
    )
```

profile of v0, /device:TPU:1, one launch (start us, length us, event | category | flops | bytes accessed | tf_op | source)
XLA Modules:
  0.0 332.2 jit_solution(8644411812769119366)
XLA Ops:
  7.2 6.4 %copy.12 = bf16[1,512,4096]{1,2,0:T(8,128)(2,1)} copy(bf16[1,512,4096]{2,1,0:T(8,128)(2,1)} %param.6) | data formatting | bytes 8388608 | tf_op args[0]
  13.6 3.9 %fusion.1 = (bf16[8,1,256,512]{2,3,0,1:T(8,128)(2,1)S(1)}, bf16[8,1,256,512]{2,3,0,1:T(8,128)(2,1)}) fusion(bf16[8,1,512,512]{2,3,0,1:T(8,128)(2,1)} %bitcast.22), kind=kLoop, calls=%fused_computation.12 | loop fusion | bytes 8388608 | tf_op jit(solution)/shard_map/split | solution.py:38
  17.4 2.4 copy.13
  19.8 8.5 %all-to-all-start = ((bf16[8,1,256,512]{3,2,1,0:T(8,128)(2,1)}), bf16[8,1,256,512]{3,2,1,0:T(8,128)(2,1)S(1)}, u32[]{:S(2)}, u32[]{:S(2)}) async-start(bf16[8,1,256,512]{3,2,1,0:T(8,128)(2,1)} %copy.13), calls=%async_computation | async-start | bytes 4194304 | tf_op jit(solution)/shard_map/all_to_all | solution.py:40
  28.3 3.9 %copy.14 = bf16[8,1,256,512]{3,2,1,0:T(8,128)(2,1)} copy(bf16[8,1,256,512]{2,3,0,1:T(8,128)(2,1)} %get-tuple-element.15) | data formatting | bytes 4194304 | tf_op jit(solution)/shard_map/split | solution.py:38
  32.2 22.3 %all-to-all-done = bf16[8,1,256,512]{3,2,1,0:T(8,128)(2,1)S(1)} async-done(((bf16[8,1,256,512]{3,2,1,0:T(8,128)(2,1)}), bf16[8,1,256,512]{3,2,1,0:T(8,128)(2,1)S(1)}, u32[]{:S(2)}, u32[]{:S(2)}) %all-to-all-start) | async-done | bytes 2097184 | tf_op jit(solution)/shard_map/all_to_all | solution.py:40
  54.5 5.2 %all-to-all-start.1 = ((bf16[8,1,256,512]{3,2,1,0:T(8,128)(2,1)}), bf16[8,1,256,512]{3,2,1,0:T(8,128)(2,1)}, u32[]{:S(2)}, u32[]{:S(2)}) async-start(bf16[8,1,256,512]{3,2,1,0:T(8,128)(2,1)} %copy.14), calls=%async_computation.1 | async-start | bytes 4194304 | tf_op jit(solution)/shard_map/all_to_all | solution.py:40
  59.7 6.4 %copy.15 = bf16[1,256,8192]{1,2,0:T(8,128)(2,1)} copy(bf16[1,256,8192]{2,1,0:T(8,128)(2,1)} %param.7) | data formatting | bytes 8388608 | tf_op args[1]
  66.0 4.6 %fusion.2 = (bf16[8,1,128,1024]{2,3,0,1:T(8,128)(2,1)}, bf16[8,1,128,1024]{2,3,0,1:T(8,128)(2,1)}) fusion(bf16[8,1,256,1024]{2,3,0,1:T(8,128)(2,1)} %bitcast.23), kind=kLoop, calls=%fused_computation.13 | loop fusion | bytes 8388608 | tf_op jit(solution)/shard_map/split | solution.py:38
  70.7 3.9 %copy.16 = bf16[8,1,128,1024]{3,2,1,0:T(8,128)(2,1)} copy(bf16[8,1,128,1024]{2,3,0,1:T(8,128)(2,1)} %get-tuple-element.16) | data formatting | bytes 4194304 | tf_op jit(solution)/shard_map/split | solution.py:38
  74.6 11.4 %all-to-all-done.1 = bf16[8,1,256,512]{3,2,1,0:T(8,128)(2,1)} async-done(((bf16[8,1,256,512]{3,2,1,0:T(8,128)(2,1)}), bf16[8,1,256,512]{3,2,1,0:T(8,128)(2,1)}, u32[]{:S(2)}, u32[]{:S(2)}) %all-to-all-start.1) | async-done | bytes 2097184 | tf_op jit(solution)/shard_map/all_to_all | solution.py:40
  86.0 5.2 %all-to-all-start.2 = ((bf16[8,1,128,1024]{3,2,1,0:T(8,128)(2,1)}), bf16[8,1,128,1024]{3,2,1,0:T(8,128)(2,1)}, u32[]{:S(2)}, u32[]{:S(2)}) async-start(bf16[8,1,128,1024]{3,2,1,0:T(8,128)(2,1)} %copy.16), calls=%async_computation.2 | async-start | bytes 4194304 | tf_op jit(solution)/shard_map/all_to_all | solution.py:40
  91.1 3.9 %copy.17 = bf16[8,1,128,1024]{3,2,1,0:T(8,128)(2,1)} copy(bf16[8,1,128,1024]{2,3,0,1:T(8,128)(2,1)} %get-tuple-element.17) | data formatting | bytes 4194304 | tf_op jit(solution)/shard_map/split | solution.py:38
  95.0 22.4 %all-to-all-done.2 = bf16[8,1,128,1024]{3,2,1,0:T(8,128)(2,1)} async-done(((bf16[8,1,128,1024]{3,2,1,0:T(8,128)(2,1)}), bf16[8,1,128,1024]{3,2,1,0:T(8,128)(2,1)}, u32[]{:S(2)}, u32[]{:S(2)}) %all-to-all-start.2) | async-done | bytes 2097184 | tf_op jit(solution)/shard_map/all_to_all | solution.py:40
  117.4 5.2 %all-to-all-start.3 = ((bf16[8,1,128,1024]{3,2,1,0:T(8,128)(2,1)}), bf16[8,1,128,1024]{3,2,1,0:T(8,128)(2,1)}, u32[]{:S(2)}, u32[]{:S(2)}) async-start(bf16[8,1,128,1024]{3,2,1,0:T(8,128)(2,1)} %copy.17), calls=%async_computation.3 | async-start | bytes 4194304 | tf_op jit(solution)/shard_map/all_to_all | solution.py:40
  122.6 0.0 all-gather.3.cloned.1.call-start
  122.6 2.3 convert_reduce_fusion.1
  124.9 0.0 copy-start
  124.9 0.9 multiply_reduce_fusion.1
  125.8 23.1 %all-to-all-done.3 = bf16[8,1,128,1024]{3,2,1,0:T(8,128)(2,1)} async-done(((bf16[8,1,128,1024]{3,2,1,0:T(8,128)(2,1)}), bf16[8,1,128,1024]{3,2,1,0:T(8,128)(2,1)}, u32[]{:S(2)}, u32[]{:S(2)}) %all-to-all-start.3) | async-done | bytes 2097184 | tf_op jit(solution)/shard_map/all_to_all | solution.py:40
  148.9 3.4 %convert_reduce_fusion = f32[256,1024]{1,0:T(8,128)S(1)} fusion(bf16[8,1,128,1024]{3,2,1,0:T(8,128)(2,1)} %all-to-all-done.3, bf16[8,1,128,1024]{3,2,1,0:T(8,128)(2,1)} %all-to-all-done.2), kind=kLoop, calls=%fused_computation | loop fusion | flops 10223616 | bytes 5242880 | tf_op jit(solution)/shard_map/reduce_sum | solution.py:71
  152.3 0.9 multiply_reduce_fusion
  154.4 5.8 %psum.35 = f32[]{:T(128)} all-reduce(f32[]{:T(128)S(6)} %add.28), channel_id=1, replica_groups=mesh['rep_0'=2,'rep_1'=4,'fsdp_0'=4,'fsdp_1'=2,'fsdp_2'=2] {'rep_0'}, use_global_device_ids=true, to_apply=%region_4.0 | all-reduce | flops 1 | bytes 8 | tf_op jit(solution)/shard_map/psum | solution.py:45
  160.2 9.0 %psum.36 = f32[]{:T(128)} all-reduce(f32[]{:T(128)} %psum.35), channel_id=1, replica_groups=mesh['rep_0'=2,'rep_1'=4,'fsdp_0'=4,'fsdp_1'=2,'fsdp_2'=2] {'rep_1'}, use_global_device_ids=true, to_apply=%region_5.0 | all-reduce | flops 1 | bytes 8 | tf_op jit(solution)/shard_map/psum | solution.py:45
  169.2 9.1 %psum.37 = f32[]{:T(128)} all-reduce(f32[]{:T(128)} %psum.36), channel_id=1, replica_groups=mesh['rep_0'=2,'rep_1'=4,'fsdp_0'=4,'fsdp_1'=2,'fsdp_2'=2] {'fsdp_0'}, use_global_device_ids=true, to_apply=%region_6.0 | all-reduce | flops 1 | bytes 8 | tf_op jit(solution)/shard_map/psum | solution.py:45
  178.3 4.4 %psum.38 = f32[]{:T(128)} all-reduce(f32[]{:T(128)} %psum.37), channel_id=1, replica_groups=mesh['rep_0'=2,'rep_1'=4,'fsdp_0'=4,'fsdp_1'=2,'fsdp_2'=2] {'fsdp_1'}, use_global_device_ids=true, to_apply=%region_7.0 | all-reduce | flops 1 | bytes 8 | tf_op jit(solution)/shard_map/psum | solution.py:45
  182.7 10.6 %psum.39 = f32[]{:T(128)} all-reduce(f32[]{:T(128)} %psum.38), channel_id=1, replica_groups=mesh['rep_0'=2,'rep_1'=4,'fsdp_0'=4,'fsdp_1'=2,'fsdp_2'=2] {'fsdp_2'}, use_global_device_ids=true, to_apply=%region_8.0 | all-reduce | flops 1 | bytes 8 | tf_op jit(solution)/shard_map/psum | solution.py:45
  193.9 0.0 copy-done
  193.9 0.0 copy-start.1
  193.9 0.0 copy-start.2
  193.9 3.1 convert_bitcast_fusion
  197.0 0.1 copy.19
  197.1 0.0 copy-done.1
  197.1 0.0 copy-done.2
  197.1 1.7 convert_bitcast_fusion.1
  198.9 0.2 copy.18
  199.1 1.0 pad_maximum_fusion
  200.1 0.0 all-gather.3.cloned.1.call-update
  200.1 100.7 %all-gather.3.cloned.1.call-done = bf16[4194304]{0:T(1024)(128)(2,1)} async-done(((bf16[524288]{0:T(1024)(128)(2,1)}), bf16[4194304]{0:T(1024)(128)(2,1)}) %all-gather.3.cloned.1.call-update) | async-done | bytes 8388624 | tf_op jit(solution)/shard_map/all_gather | solution.py:50
  300.9 10.1 %reshape.48 = bf16[8,524288]{1,0:T(8,128)(2,1)} reshape(bf16[4194304]{0:T(1024)(128)(2,1)} %all-gather.3.cloned.1.call-done) | data formatting | bytes 16777216 | tf_op jit(solution)/shard_map/all_gather | solution.py:50
  311.0 3.8 %fusion = (bf16[8,262144]{1,0:T(8,128)(2,1)S(1)}, bf16[8,262144]{1,0:T(8,128)(2,1)S(1)}) fusion(bf16[8,524288]{1,0:T(8,128)(2,1)} %reshape.48), kind=kLoop, calls=%fused_computation.11 | loop fusion | bytes 16777216 | tf_op jit(solution)/shard_map/slice | solution.py:52
  314.8 6.3 %copy.21 = bf16[32,8,8,1024]{3,1,2,0:T(8,128)(2,1)} copy(bf16[32,8,8,1024]{3,2,1,0:T(8,128)(2,1)S(1)} %bitcast.25) | data formatting | bytes 8388608
  321.1 4.2 %copy.20 = bf16[64,8,8,512]{3,1,2,0:T(8,128)(2,1)} copy(bf16[64,8,8,512]{3,2,1,0:T(8,128)(2,1)S(1)} %bitcast.24) | data formatting | bytes 8388608
Async XLA Ops:
  19.8 34.7 %all-to-all-start = ((bf16[8,1,256,512]{3,2,1,0:T(8,128)(2,1)}), bf16[8,1,256,512]{3,2,1,0:T(8,128)(2,1)S(1)}, u32[]{:S(2)}, u32[]{:S(2)}) async-start(bf16[8,1,256,512]{3,2,1,0:T(8,128)(2,1)} %copy.13), calls=%async_computation | async-start | bytes 4194304 | tf_op jit(solution)/shard_map/all_to_all | solution.py:40
  54.5 31.5 %all-to-all-start.1 = ((bf16[8,1,256,512]{3,2,1,0:T(8,128)(2,1)}), bf16[8,1,256,512]{3,2,1,0:T(8,128)(2,1)}, u32[]{:S(2)}, u32[]{:S(2)}) async-start(bf16[8,1,256,512]{3,2,1,0:T(8,128)(2,1)} %copy.14), calls=%async_computation.1 | async-start | bytes 4194304 | tf_op jit(solution)/shard_map/all_to_all | solution.py:40
  86.0 31.5 %all-to-all-start.2 = ((bf16[8,1,128,1024]{3,2,1,0:T(8,128)(2,1)}), bf16[8,1,128,1024]{3,2,1,0:T(8,128)(2,1)}, u32[]{:S(2)}, u32[]{:S(2)}) async-start(bf16[8,1,128,1024]{3,2,1,0:T(8,128)(2,1)} %copy.16), calls=%async_computation.2 | async-start | bytes 4194304 | tf_op jit(solution)/shard_map/all_to_all | solution.py:40
  117.4 31.5 %all-to-all-start.3 = ((bf16[8,1,128,1024]{3,2,1,0:T(8,128)(2,1)}), bf16[8,1,128,1024]{3,2,1,0:T(8,128)(2,1)}, u32[]{:S(2)}, u32[]{:S(2)}) async-start(bf16[8,1,128,1024]{3,2,1,0:T(8,128)(2,1)} %copy.17), calls=%async_computation.3 | async-start | bytes 4194304 | tf_op jit(solution)/shard_map/all_to_all | solution.py:40
  122.6 178.3 %all-gather.3.cloned.1.call-start = ((), (), s32[]{:S(2)}) async-start(), calls=%async_computation.4 | async-start | bytes 9437184 | tf_op jit(solution)/shard_map/all_gather | solution.py:50
  124.9 69.0 %copy-start = (f32[256,1024]{1,0:T(8,128)S(1)}, f32[256,1024]{1,0:T(8,128)}, u32[]{:S(2)}) copy-start(f32[256,1024]{1,0:T(8,128)} %param.9) | copy-start | bytes 3145732
  193.9 3.2 copy-start.1
  193.9 3.2 copy-start.2
Sparse Core Ops, SparseCore 0:
  200.3 100.5 all-gather.2
where the time goes:
time: 333 us; the launch traced here: 332 us
  waiting for transfers between devices  180 us (54%)
  local copies, waits for them, and re-layouts  60.2 us (18%)
  blocking collectives  38.8 us (12%)
  starting transfers between devices  24 us (7%)
  between operations  16.1 us (5%)
  other arithmetic  13.2 us (4%)
    all_gather x1, waiting for transfers between devices, one_gather(): lines, at, done = (lax.all_gather(line, axis), 0, [])  101 us
    all_to_all x4, waiting for transfers between devices, several_exchanges(): lax.all_to_all(share, axis, split_axis=0, concat_axis=0, tiled=True)  79.1 us
    psum x5, blocking collectives, by_axis(): return functools.reduce(lax.psum, axes, value)  38.8 us
    all_to_all x4, starting transfers between devices, several_exchanges(): lax.all_to_all(share, axis, split_axis=0, concat_axis=0, tiled=True)  23.9 us
    unnamed x12, local copies, waits for them, and re-layouts  23.7 us
    split x6, local copies, waits for them, and re-layouts, several_exchanges(): jnp.split(parts, cut_rows(parts.shape[widest], pieces), axis=widest)  22.7 us
    all_gather x1, local copies, waits for them, and re-layouts, one_gather(): lines, at, done = (lax.all_gather(line, axis), 0, [])  10.1 us
  transfers between devices with their start and end apart: 5, of which 5 were waited for; matrix products, arithmetic and copies ran while one was open for 8% of the time, Pallas kernels for 0%

commit v1 on v0

v1 whole, which is shorter than its diff:
```python
import functools
import math

import jax
import jax.numpy as jnp
from jax import lax
from jax.experimental import pallas as pl
from jax.experimental.pallas import tpu as pltpu
from jax.sharding import PartitionSpec as P

MESH = pl.DeviceIdType.MESH
BF16, F32 = jnp.bfloat16, jnp.float32
LIMIT = 0.25 * math.sqrt(2.0 * 8192 * 4096)
FIRST_Z = 9 / 16
STEP = 16


class Part:
    def __init__(self, rows, columns, sign):
        self.rows, self.columns, self.sign = rows, columns, sign
        self.a = int(rows * FIRST_Z) // STEP * STEP
        self.b = rows - self.a

    def window(self, owner):
        return pl.ds(pl.multiple_of(owner * self.columns, self.columns), self.columns)


def over_rows(rows, body, carry=None):
    def step(i, carry):
        return body(pl.ds(pl.multiple_of(i * STEP, STEP), STEP), carry)

    return lax.fori_loop(0, rows // STEP, step, carry, unroll=2 if rows // STEP % 2 == 0 else 1)


def add_up(out, *terms):
    def body(rows, _):
        total = terms[0][rows, :].astype(F32)
        for term in terms[1:]:
            total = total + term[rows, :].astype(F32)
        out[rows, :] = total.astype(out.dtype)

    over_rows(out.shape[0], body)


def add_up_squares(out, *terms):
    def body(rows, squares):
        total = terms[0][rows, :].astype(F32)
        for term in terms[1:]:
            total = total + term[rows, :].astype(F32)
        out[rows, :] = total
        return squares + total * total

    columns = out.shape[1]
    squares = over_rows(out.shape[0], body, jnp.zeros((STEP, columns), F32))
    line = jnp.sum(squares, axis=0, keepdims=True)
    return functools.reduce(jnp.add, [line[:, k : k + 128] for k in range(0, columns, 128)])


def kernel(parts, *refs):
    delta, master, moment = refs[0:2], refs[2:4], refs[4:6]
    weights, master_next, moment_next = refs[6:8], refs[8:10], refs[10:12]
    at = 12
    bufs = []
    for p in parts:
        names = list(shapes(p))
        bufs.append(dict(zip(names, refs[at : at + len(names)])))
        at += len(names)
    line1, line2, send_sem, recv_sem, local_sem = refs[at:]

    rep, shard = lax.axis_index("rep"), lax.axis_index("fsdp")
    y_hi, z = rep // 4, lax.rem(rep, 4)
    x, y_lo, core = shard // 4, lax.rem(shard // 2, 2), lax.rem(shard, 2)

    def owner(across, dz):
        return (1 - y_hi if across else y_hi) * 4 + lax.rem(z + dz % 4, 4)

    def chip(dx=0, dy=0, dz=0, dc=0):
        y = lax.rem(y_hi * 2 + y_lo + dy, 4)
        there = lax.rem(x + dx, 4) * 4 + lax.rem(y, 2) * 2 + lax.rem(core + dc, 2)
        return (y // 2) * 4 + lax.rem(z + dz, 4), there

    flying, local = {}, []

    def send(key, src, dst, target):
        k = len(flying)
        flying[key] = pltpu.make_async_remote_copy(
            src, dst, send_sem.at[k], recv_sem.at[k], device_id=target, device_id_type=MESH
        )
        flying[key].start()

    def arrived(*key):
        flying[key].wait_recv()

    def along_z(key, src, dst, dz):
        send(key, src, dst, (owner(0, dz), shard))

    def along_y(key, src, dst):
        send(key, src, dst, (owner(1, 0), shard))

    def start_local(src, dst):
        copy = pltpu.make_async_copy(src, dst, local_sem.at[len(local)])
        copy.start()
        local.append(copy)
        return copy

    both = range(len(parts))
    rows_a = [pl.ds(0, p.a) for p in parts]
    rows_b = [pl.ds(p.a, p.b) for p in parts]
    s = [p.sign for p in parts]

    own_a, own_b, params = {}, {}, []
    for side in (0, 1):
        for j in (0, 1):
            for t in both:
                cut = delta[t].at[rows_a[t], parts[t].window(owner(1 - side, (1 - j) * s[t]))]
                own_a[t, j, side] = start_local(cut, bufs[t]["own_a"].at[j, side])
    for k in range(4):
        for t in both:
            cut = delta[t].at[rows_b[t], parts[t].window(owner(0, k * s[t]))]
            own_b[t, k] = start_local(cut, bufs[t]["own_b"].at[k])
    for t in both:
        params.append(start_local(master[t], bufs[t]["master"]))
        params.append(start_local(moment[t], bufs[t]["moment"]))

    plane = [(dy, dz) for dy in range(4) for dz in range(4)][1:]
    across = [(dx, dc) for dx in range(4) for dc in range(2)][1:]
    barrier = pltpu.get_barrier_semaphore()
    for dy, dz in plane:
        pl.semaphore_signal(barrier, inc=1, device_id=chip(dy=dy, dz=dz), device_id_type=MESH)
    for dx, dc in across:
        pl.semaphore_signal(barrier, inc=1, device_id=chip(dx=dx, dc=dc), device_id_type=MESH)
    pl.semaphore_wait(barrier, len(plane) + len(across))

    def raw_a(side, t):
        p, b = parts[t], bufs[t]
        src = delta[t].at[rows_a[t], p.window(owner(1 - side, 2))]
        along_z(("a2", side, t), src, b["a2"].at[side], s[t])

    def raw_a_alone(side, t):
        p, b = parts[t], bufs[t]
        src = delta[t].at[rows_a[t], p.window(owner(1 - side, -s[t]))]
        along_z(("a1", side, t), src, b["a1"].at[side], -s[t])

    def merge_a(side, t):
        b = bufs[t]
        arrived("a2", side, t)
        own_a[t, 0, side].wait()
        add_up(b["merged_a"].at[side], b["own_a"].at[0, side], b["a2"].at[side])
        along_z(("am", side, t), b["merged_a"].at[side], b["am"].at[side], s[t])

    def raw_b(k, t):
        p, b = parts[t], bufs[t]
        src = delta[t].at[rows_b[t], p.window(owner(1, k * s[t]))]
        along_y(("by", k, t), src, b["by"].at[k])

    for t in both:
        raw_a(0, t)
    for t in both:
        raw_b(2, t)
    for t in both:
        raw_a_alone(0, t)
    for k in (3, 1):
        for t in both:
            raw_b(k, t)
    for t in both:
        merge_a(0, t)
    for t in both:
        raw_a(1, t)
    for t in both:
        raw_a_alone(1, t)
    for t in both:
        b = bufs[t]
        arrived("by", 2, t)
        own_b[t, 2].wait()
        add_up(b["sum_b"].at[0], b["own_b"].at[2], b["by"].at[2])
        along_z(("b2", t), b["sum_b"].at[0], b["b2"], s[t])
    for t in both:
        b = bufs[t]
        arrived("by", 3, t)
        own_b[t, 3].wait()
        add_up(b["sum_b"].at[1], b["own_b"].at[3], b["by"].at[3])
        along_z(("b1", t), b["sum_b"].at[1], b["b1"], -s[t])
    for t in both:
        b = bufs[t]
        arrived("a1", 0, t)
        arrived("am", 0, t)
        own_a[t, 1, 0].wait()
        add_up(b["sum_a"], b["own_a"].at[1, 0], b["a1"].at[0], b["am"].at[0])
        along_y(("ay", t), b["sum_a"], b["ay"])
    for t in both:
        raw_b(0, t)
    for t in both:
        merge_a(1, t)
    for t in both:
        b = bufs[t]
        arrived("by", 1, t)
        arrived("b2", t)
        own_b[t, 1].wait()
        add_up(b["sum_b"].at[2], b["own_b"].at[1], b["by"].at[1], b["b2"])
        along_z(("bm", t), b["sum_b"].at[2], b["bm"], s[t])

    for copy in params:
        copy.wait()
    for t in both:
        b = bufs[t]

        def base(rows, _, b=b):
            b["master"][rows, :] = b["master"][rows, :] - 0.567 * b["moment"][rows, :]

        over_rows(parts[t].rows, base)

    line = jnp.zeros((1, 128), F32)
    for t in both:
        b, p = bufs[t], parts[t]
        arrived("a1", 1, t)
        arrived("am", 1, t)
        arrived("ay", t)
        own_a[t, 1, 1].wait()
        terms = (b["own_a"].at[1, 1], b["a1"].at[1], b["am"].at[1], b["ay"])
        line += add_up_squares(b["total"].at[rows_a[t]], *terms)
    for t in both:
        b, p = bufs[t], parts[t]
        arrived("by", 0, t)
        arrived("b1", t)
        arrived("bm", t)
        own_b[t, 0].wait()
        terms = (b["own_b"].at[0], b["by"].at[0], b["b1"], b["bm"])
        line += add_up_squares(b["total"].at[rows_b[t]], *terms)

    line1[pl.ds(0, 1)] = line
    for i, (dy, dz) in enumerate(plane):
        send(("n1", i), line1.at[pl.ds(0, 1)], line1.at[pl.ds(i + 1, 1)], chip(dy=dy, dz=dz))
    for i in range(len(plane)):
        arrived("n1", i)
    line2[pl.ds(0, 1)] = jnp.sum(line1[...], axis=0, keepdims=True)
    for i, (dx, dc) in enumerate(across):
        send(("n2", i), line2.at[pl.ds(0, 1)], line2.at[pl.ds(i + 1, 1)], chip(dx=dx, dc=dc))
    for i in range(len(across)):
        arrived("n2", i)
    square_sum = jnp.sum(line2[...], axis=(0, 1), keepdims=True) * (1.0 / 64.0)
    factor = jnp.minimum(1.0, LIMIT / jnp.sqrt(square_sum + 1e-06)) * 0.125

    def update(t, first, rows_here):
        b = bufs[t]
        scale = 1.33 * factor

        def body(rows, _):
            rows = pl.ds(pl.multiple_of(first + rows.start, STEP), STEP)
            new = b["master"][rows, :] - scale * b["total"][rows, :]
            b["master"][rows, :] = new
            b["weights"][rows, :] = new.astype(BF16)

        over_rows(rows_here, body)

    def out_at(t, rows, who):
        return weights[t].at[rows, parts[t].window(who)]

    def give(t, rows, dz, who, src=None):
        key = ("w", t, rows is rows_a[t], dz, who)
        dst = out_at(t, rows, owner(*who))
        src = dst if src is None else src
        if dz is None:
            along_y(key, src, dst)
        else:
            along_z(key, src, dst, dz)

    def got(t, rows, dz, who):
        arrived("w", t, rows is rows_a[t], dz, who)

    own = (0, 0)
    for t in both:
        update(t, 0, parts[t].a)
        give(t, rows_a[t], None, own, bufs[t]["weights"].at[rows_a[t]])
    for t in both:
        update(t, parts[t].a, parts[t].b)
        for dz in (s[t], -s[t]):
            give(t, rows_b[t], dz, own, bufs[t]["weights"].at[rows_b[t]])
    for t in both:
        give(t, rows_b[t], None, own, bufs[t]["weights"].at[rows_b[t]])
    for t in both:
        for dz in (s[t], -s[t]):
            give(t, rows_a[t], dz, own, bufs[t]["weights"].at[rows_a[t]])
    for t in both:
        start_local(bufs[t]["weights"], weights[t].at[:, parts[t].window(rep)])
        start_local(bufs[t]["master"], master_next[t])

    def next_moment(t):
        b = bufs[t]

        def body(rows, _):
            b["moment"][rows, :] = 0.9 * b["moment"][rows, :] + factor * b["total"][rows, :]

        over_rows(parts[t].rows, body)
        start_local(b["moment"], moment_next[t])

    for t in both:
        got(t, rows_b[t], s[t], own)
        give(t, rows_b[t], s[t], (0, -s[t]))
        give(t, rows_b[t], None, (0, -s[t]))
    for t in both:
        got(t, rows_b[t], -s[t], own)
        give(t, rows_b[t], None, (0, s[t]))
    for t in both:
        next_moment(t)
    for t in both:
        got(t, rows_a[t], None, own)
        for dz in (s[t], -s[t]):
            give(t, rows_a[t], dz, (1, 0))
    for t in both:
        got(t, rows_b[t], s[t], (0, -s[t]))
        give(t, rows_b[t], None, (0, 2))
    for t in both:
        got(t, rows_a[t], s[t], own)
        give(t, rows_a[t], s[t], (0, -s[t]))
    for t in both:
        got(t, rows_a[t], s[t], (1, 0))
        give(t, rows_a[t], s[t], (1, -s[t]))
    for t in both:
        got(t, rows_a[t], -s[t], own)
        got(t, rows_a[t], -s[t], (1, 0))
        got(t, rows_a[t], s[t], (0, -s[t]))
        got(t, rows_a[t], s[t], (1, -s[t]))
        for who in (own, (0, -s[t]), (0, s[t]), (0, 2)):
            got(t, rows_b[t], None, who)
    for copy in flying.values():
        copy.wait_send()
    for copy in local[-6:]:
        copy.wait()


def shapes(p):
    a, b, c = p.a, p.b, p.columns
    return {
        "own_a": (2, 2, a, c),
        "own_b": (4, b, c),
        "a2": (2, a, c),
        "a1": (2, a, c),
        "am": (2, a, c),
        "ay": (a, c),
        "merged_a": (2, a, c),
        "sum_a": (a, c),
        "by": (4, b, c),
        "b2": (b, c),
        "b1": (b, c),
        "bm": (b, c),
        "sum_b": (3, b, c),
        "total": (p.rows, c),
        "master": (p.rows, c),
        "moment": (p.rows, c),
        "weights": (p.rows, c),
    }


def scratch(p):
    wide = ("total", "master", "moment")
    return [pltpu.VMEM(shape, F32 if n in wide else BF16) for n, shape in shapes(p).items()]


def on_device(delta_query, delta_output, *params):
    deltas = (delta_query[0], delta_output[0])
    parts = (Part(*params[0].shape, 1), Part(*params[1].shape, -1))
    outs = [jax.ShapeDtypeStruct(d.shape, BF16) for d in deltas]
    outs += [jax.ShapeDtypeStruct(p.shape, F32) for p in params]
    anywhere = pl.BlockSpec(memory_space=pl.ANY)
    return pl.pallas_call(
        functools.partial(kernel, parts),
        out_shape=outs,
        in_specs=[anywhere] * 6,
        out_specs=[anywhere] * 6,
        scratch_shapes=[
            *scratch(parts[0]),
            *scratch(parts[1]),
            pltpu.VMEM((16, 128), F32),
            pltpu.VMEM((8, 128), F32),
            pltpu.SemaphoreType.DMA((80,)),
            pltpu.SemaphoreType.DMA((80,)),
            pltpu.SemaphoreType.DMA((32,)),
        ],
        compiler_params=pltpu.CompilerParams(collective_id=0, has_side_effects=True),
        name="outer_step",
    )(*deltas, *params)


def solution(mesh):
    placed = P("fsdp", "rep")
    return jax.shard_map(
        on_device,
        mesh=mesh,
        in_specs=(P("rep", "fsdp", None),) * 2 + (placed,) * 4,
        out_specs=(P("fsdp", None),) * 2 + (placed,) * 4,
        check_vma=False,
    )
```

time: 333 us -> 140 us (0.42)
  waiting for transfers between devices: 180 us -> 0 us
  Pallas kernels: 0 us -> 128 us
  local copies, waits for them, and re-layouts: 60.2 us -> 10.9 us
  blocking collectives: 38.8 us -> 0 us
  starting transfers between devices: 24 us -> 0 us
  between operations: 16.1 us -> 0.66 us
  other arithmetic: 13.2 us -> 0 us
    pallas_call x0 -> x1, Pallas kernels: none -> 128 us  [on_device(): pl.pallas_call(functools.partial(kernel, parts), out_shape=outs, in_specs...]
    all_gather x1 -> x0, waiting for transfers between devices: 101 us -> none  [one_gather(): lines, at, done = (lax.all_gather(line, axis), 0, [])]
    all_to_all x4 -> x0, waiting for transfers between devices: 79.1 us -> none  [several_exchanges(): lax.all_to_all(share, axis, split_axis=0, concat_axis=0, tiled=True)]
    psum x5 -> x0, blocking collectives: 38.8 us -> none  [by_axis(): return functools.reduce(lax.psum, axes, value)]
    all_to_all x4 -> x0, starting transfers between devices: 23.9 us -> none  [several_exchanges(): lax.all_to_all(share, axis, split_axis=0, concat_axis=0, tiled=True)]
    split x6 -> x0, local copies, waits for them, and re-layouts: 22.7 us -> none  [several_exchanges(): jnp.split(parts, cut_rows(parts.shape[widest], pieces), axis=widest)]
    unnamed x12 -> x16, local copies, waits for them, and re-layouts: 23.7 us -> 10.9 us
    all_gather x1 -> x0, local copies, waits for them, and re-layouts: 10.1 us -> none  [one_gather(): lines, at, done = (lax.all_gather(line, axis), 0, [])]
  transfers between devices with their start and end apart: 5 -> 0, of which waited for: 5 -> 0; matrix products, arithmetic and copies ran while one was open for 8% -> 0% of each run, Pallas kernels for 0% -> 0%
where the time goes in v1:
time: 140 us
  Pallas kernels  128 us (91%)
  local copies, waits for them, and re-layouts  10.9 us (8%)
    pallas_call x1, Pallas kernels, on_device(): pl.pallas_call(functools.partial(kernel, parts), out_shape=outs, in_specs...  128 us
    unnamed x16, local copies, waits for them, and re-layouts  10.9 us

profile of v1, /device:TPU:1, one launch (start us, length us, event | category | flops | bytes accessed | tf_op | source)
XLA Modules:
  0.0 140.0 jit_solution(15787376067472189088)
XLA Ops:
  0.6 128.5 %outer_step.1 = (bf16[512,4096]{1,0:T(8,128)(2,1)}, bf16[256,8192]{1,0:T(8,128)(2,1)}, f32[512,512]{1,0:T(8,128)}, f32[256,1024]{1,0:T(8,128)}, f32[512,512]{1,0:T(8,128)}, /*index=5*/f32[256,1024]{1,0:T(8,128)}) custom-call(bf16[512,4096]{1,0:T(8,128)(2,1)} %bitcast.2, bf16[256,8192]{1,0:T(8,128)(2,1)} %bitcast.3, f32[512,512]{1,0:T(8,128)} %refs_2_.1, ...), custom_call_target="tpu_custom_call" | custom-call | tf_op jit(solution)/shard_map/outer_step/pallas_call | solution.py:365
  129.1 0.0 copy-start
  129.1 4.8 %copy.18 = bf16[512,4096]{1,0:T(8,128)(2,1)} copy(bf16[512,4096]{1,0:T(8,128)(2,1)} %get-tuple-element.12) | data formatting | bytes 8388608
  134.0 0.0 copy-done
  134.0 0.0 copy-start.4
  134.0 0.0 copy-start.3
  134.0 2.1 %copy.19 = bf16[256,8192]{1,0:T(8,128)(2,1)} copy(bf16[256,8192]{1,0:T(8,128)(2,1)S(1)} %copy-done) | data formatting | bytes 8388608
  136.1 0.0 copy-done.4
  136.1 0.0 copy-start.2
  136.1 0.0 copy-start.1
  136.1 1.0 copy.20
  137.1 0.0 copy-done.3
  137.1 1.0 copy.21
  138.1 0.0 copy-done.2
  138.1 1.0 copy.22
  139.1 0.0 copy-done.1
  139.1 1.0 copy.23
Async XLA Ops:
  129.1 4.9 %copy-start = (bf16[256,8192]{1,0:T(8,128)(2,1)S(1)}, bf16[256,8192]{1,0:T(8,128)(2,1)}, u32[]{:S(2)}) copy-start(bf16[256,8192]{1,0:T(8,128)(2,1)} %get-tuple-element.13) | copy-start | bytes 12582916
  134.0 2.1 %copy-start.4 = (f32[512,512]{1,0:T(8,128)S(1)}, f32[512,512]{1,0:T(8,128)}, u32[]{:S(2)}) copy-start(f32[512,512]{1,0:T(8,128)} %get-tuple-element.14) | copy-start | bytes 3145732
  134.0 3.1 %copy-start.3 = (f32[256,1024]{1,0:T(8,128)S(1)}, f32[256,1024]{1,0:T(8,128)}, u32[]{:S(2)}) copy-start(f32[256,1024]{1,0:T(8,128)} %get-tuple-element.15) | copy-start | bytes 3145732
  136.1 1.9 %copy-start.2 = (f32[512,512]{1,0:T(8,128)S(1)}, f32[512,512]{1,0:T(8,128)}, u32[]{:S(2)}) copy-start(f32[512,512]{1,0:T(8,128)} %get-tuple-element.16) | copy-start | bytes 3145732
  136.1 2.9 %copy-start.1 = (f32[256,1024]{1,0:T(8,128)S(1)}, f32[256,1024]{1,0:T(8,128)}, u32[]{:S(2)}) copy-start(f32[256,1024]{1,0:T(8,128)} %get-tuple-element.17) | copy-start | bytes 3145732

commit v2 on v1

--- a/solution.py
+++ b/solution.py
@@ -119,8 +119,8 @@
             cut = delta[t].at[rows_b[t], parts[t].window(owner(0, k * s[t]))]
             own_b[t, k] = start_local(cut, bufs[t]["own_b"].at[k])
     for t in both:
-        params.append(start_local(master[t], bufs[t]["master"]))
-        params.append(start_local(moment[t], bufs[t]["moment"]))
+        params.append(start_local(master[t], master_next[t]))
+        params.append(start_local(moment[t], moment_next[t]))
 
     plane = [(dy, dz) for dy in range(4) for dz in range(4)][1:]
     across = [(dx, dc) for dx in range(4) for dc in range(2)][1:]
@@ -202,10 +202,9 @@
     for copy in params:
         copy.wait()
     for t in both:
-        b = bufs[t]
-
-        def base(rows, _, b=b):
-            b["master"][rows, :] = b["master"][rows, :] - 0.567 * b["moment"][rows, :]
+
+        def base(rows, _, t=t):
+            master_next[t][rows, :] = master_next[t][rows, :] - 0.567 * moment_next[t][rows, :]
 
         over_rows(parts[t].rows, base)
 
@@ -243,26 +242,26 @@
     def update(t, first, rows_here):
         b = bufs[t]
         scale = 1.33 * factor
+        mine = parts[t].window(rep)
 
         def body(rows, _):
             rows = pl.ds(pl.multiple_of(first + rows.start, STEP), STEP)
-            new = b["master"][rows, :] - scale * b["total"][rows, :]
-            b["master"][rows, :] = new
-            b["weights"][rows, :] = new.astype(BF16)
+            new = master_next[t][rows, :] - scale * b["total"][rows, :]
+            master_next[t][rows, :] = new
+            weights[t][rows, mine] = new.astype(BF16)
 
         over_rows(rows_here, body)
 
     def out_at(t, rows, who):
         return weights[t].at[rows, parts[t].window(who)]
 
-    def give(t, rows, dz, who, src=None):
+    def give(t, rows, dz, who):
         key = ("w", t, rows is rows_a[t], dz, who)
-        dst = out_at(t, rows, owner(*who))
-        src = dst if src is None else src
+        place = out_at(t, rows, owner(*who))
         if dz is None:
-            along_y(key, src, dst)
+            along_y(key, place, place)
         else:
-            along_z(key, src, dst, dz)
+            along_z(key, place, place, dz)
 
     def got(t, rows, dz, who):
         arrived("w", t, rows is rows_a[t], dz, who)
@@ -270,28 +269,24 @@
     own = (0, 0)
     for t in both:
         update(t, 0, parts[t].a)
-        give(t, rows_a[t], None, own, bufs[t]["weights"].at[rows_a[t]])
+        give(t, rows_a[t], None, own)
     for t in both:
         update(t, parts[t].a, parts[t].b)
         for dz in (s[t], -s[t]):
-            give(t, rows_b[t], dz, own, bufs[t]["weights"].at[rows_b[t]])
-    for t in both:
-        give(t, rows_b[t], None, own, bufs[t]["weights"].at[rows_b[t]])
+            give(t, rows_b[t], dz, own)
+    for t in both:
+        give(t, rows_b[t], None, own)
     for t in both:
         for dz in (s[t], -s[t]):
-            give(t, rows_a[t], dz, own, bufs[t]["weights"].at[rows_a[t]])
-    for t in both:
-        start_local(bufs[t]["weights"], weights[t].at[:, parts[t].window(rep)])
-        start_local(bufs[t]["master"], master_next[t])
+            give(t, rows_a[t], dz, own)
 
     def next_moment(t):
-        b = bufs[t]
+        b, m = bufs[t], moment_next[t]
 
         def body(rows, _):
-            b["moment"][rows, :] = 0.9 * b["moment"][rows, :] + factor * b["total"][rows, :]
+            m[rows, :] = 0.9 * m[rows, :] + factor * b["total"][rows, :]
 
         over_rows(parts[t].rows, body)
-        start_local(b["moment"], moment_next[t])
 
     for t in both:
         got(t, rows_b[t], s[t], own)
@@ -324,8 +319,6 @@
             got(t, rows_b[t], None, who)
     for copy in flying.values():
         copy.wait_send()
-    for copy in local[-6:]:
-        copy.wait()
 
 
 def shapes(p):
@@ -345,28 +338,33 @@
         "bm": (b, c),
         "sum_b": (3, b, c),
         "total": (p.rows, c),
-        "master": (p.rows, c),
-        "moment": (p.rows, c),
-        "weights": (p.rows, c),
     }
 
 
 def scratch(p):
-    wide = ("total", "master", "moment")
-    return [pltpu.VMEM(shape, F32 if n in wide else BF16) for n, shape in shapes(p).items()]
+    return [pltpu.VMEM(shape, F32 if n == "total" else BF16) for n, shape in shapes(p).items()]
+
+
+def write_out(*refs):
+    count = len(refs) // 2
+    copies = [pltpu.make_async_copy(refs[i], refs[count + i], refs[-1].at[i]) for i in range(count)]
+    for copy in copies:
+        copy.start()
+    for copy in copies:
+        copy.wait()
 
 
 def on_device(delta_query, delta_output, *params):
     deltas = (delta_query[0], delta_output[0])
     parts = (Part(*params[0].shape, 1), Part(*params[1].shape, -1))
-    outs = [jax.ShapeDtypeStruct(d.shape, BF16) for d in deltas]
-    outs += [jax.ShapeDtypeStruct(p.shape, F32) for p in params]
-    anywhere = pl.BlockSpec(memory_space=pl.ANY)
-    return pl.pallas_call(
+    outs = [(d.shape, BF16) for d in deltas] + [(p.shape, F32) for p in params]
+    in_hbm = pl.BlockSpec(memory_space=pltpu.HBM)
+    in_vmem = pl.BlockSpec(memory_space=pltpu.VMEM)
+    held = pl.pallas_call(
         functools.partial(kernel, parts),
-        out_shape=outs,
-        in_specs=[anywhere] * 6,
-        out_specs=[anywhere] * 6,
+        out_shape=[pltpu.VMEM(*out) for out in outs],
+        in_specs=[in_hbm] * 6,
+        out_specs=[in_vmem] * 6,
         scratch_shapes=[
             *scratch(parts[0]),
             *scratch(parts[1]),
@@ -376,9 +374,20 @@
             pltpu.SemaphoreType.DMA((80,)),
             pltpu.SemaphoreType.DMA((32,)),
         ],
-        compiler_params=pltpu.CompilerParams(collective_id=0, has_side_effects=True),
+        compiler_params=pltpu.CompilerParams(
+            collective_id=0, has_side_effects=True, vmem_limit_bytes=44 << 20
+        ),
         name="outer_step",
     )(*deltas, *params)
+    return pl.pallas_call(
+        write_out,
+        out_shape=[jax.ShapeDtypeStruct(*out) for out in outs],
+        in_specs=[in_vmem] * 6,
+        out_specs=[in_hbm] * 6,
+        scratch_shapes=[pltpu.SemaphoreType.DMA((6,))],
+        compiler_params=pltpu.CompilerParams(vmem_limit_bytes=16 << 20),
+        name="write_out",
+    )(*held)
 
 
 def solution(mesh):

time: 140 us -> 134 us (0.957)
  local copies, waits for them, and re-layouts: 10.9 us -> 0 us
  Pallas kernels: 128 us -> 133 us
    unnamed x16 -> x0, local copies, waits for them, and re-layouts: 10.9 us -> none
    pallas_call x1 -> x2, Pallas kernels: 128 us -> 133 us  [the longest x1 128 us: on_device(): pl.pallas_call(functools.partial(kernel, parts), out_shape=[pltpu.VMEM(*o...]
where the time goes in v2:
time: 134 us
  Pallas kernels  133 us (99%)
    pallas_call x1, Pallas kernels, on_device(): pl.pallas_call(functools.partial(kernel, parts), out_shape=[pltpu.VMEM(*o...  128 us
    pallas_call x1, Pallas kernels, on_device(): pl.pallas_call(write_out, out_shape=[jax.ShapeDtypeStruct(*out) for out i...  4.61 us

profile of v2, /device:TPU:1, one launch (start us, length us, event | category | flops | bytes accessed | tf_op | source)
XLA Modules:
  0.0 133.6 jit_solution(1175051540837185169)
XLA Ops:
  0.6 128.4 %outer_step.1 = (bf16[512,4096]{1,0:T(8,128)(2,1)S(1)}, bf16[256,8192]{1,0:T(8,128)(2,1)S(1)}, f32[512,512]{1,0:T(8,128)S(1)}, f32[256,1024]{1,0:T(8,128)S(1)}, ...) custom-call(bf16[512,4096]{1,0:T(8,128)(2,1)} %bitcast.2, bf16[256,8192]{1,0:T(8,128)(2,1)} %bitcast.3, ...), custom_call_target="tpu_custom_call" | custom-call | tf_op jit(solution)/shard_map/outer_step/pallas_call | solution.py:363
  129.0 4.6 %write_out.1 = (bf16[512,4096]{1,0:T(8,128)(2,1)}, bf16[256,8192]{1,0:T(8,128)(2,1)}, f32[512,512]{1,0:T(8,128)}, f32[256,1024]{1,0:T(8,128)}, f32[512,512]{1,0:T(8,128)}, /*index=5*/f32[256,1024]{1,0:T(8,128)}) custom-call(bf16[512,4096]{1,0:T(8,128)(2,1)S(1)} %get-tuple-element.12.refs_0_, bf16[256,8192]{1,0:T(8,128)(2,1)S(1)} %get-tuple-element.13.refs_1_, ...), custom_call_target="tpu_custom_call" | custom-call | tf_op jit(solution)/shard_map/write_out/pallas_call | solution.py:382

commit v3 on v2

--- a/solution.py
+++ b/solution.py
@@ -12,6 +12,7 @@
 BF16, F32 = jnp.bfloat16, jnp.float32
 LIMIT = 0.25 * math.sqrt(2.0 * 8192 * 4096)
 FIRST_Z = 9 / 16
+EARLY = 3 / 16
 STEP = 16
 
 
@@ -20,6 +21,7 @@
         self.rows, self.columns, self.sign = rows, columns, sign
         self.a = int(rows * FIRST_Z) // STEP * STEP
         self.b = rows - self.a
+        self.g = int(rows * EARLY) // STEP * STEP
 
     def window(self, owner):
         return pl.ds(pl.multiple_of(owner * self.columns, self.columns), self.columns)
@@ -106,7 +108,50 @@
     both = range(len(parts))
     rows_a = [pl.ds(0, p.a) for p in parts]
     rows_b = [pl.ds(p.a, p.b) for p in parts]
+    rows_g = [pl.ds(0, p.g) for p in parts]
+    rows_h = [pl.ds(p.g, p.a - p.g) for p in parts]
     s = [p.sign for p in parts]
+
+    plane = [(dy, dz) for dy in range(4) for dz in range(4)][1:]
+    across = [(dx, dc) for dx in range(4) for dc in range(2)][1:]
+    barrier = pltpu.get_barrier_semaphore()
+    for dy, dz in plane:
+        pl.semaphore_signal(barrier, inc=1, device_id=chip(dy=dy, dz=dz), device_id_type=MESH)
+    for dx, dc in across:
+        pl.semaphore_signal(barrier, inc=1, device_id=chip(dx=dx, dc=dc), device_id_type=MESH)
+    pl.semaphore_wait(barrier, len(plane) + len(across))
+
+    def raw_a(side, t):
+        p, b = parts[t], bufs[t]
+        src = delta[t].at[rows_a[t], p.window(owner(1 - side, 2))]
+        along_z(("a2", side, t), src, b["a2"].at[side], s[t])
+
+    def raw_a_alone(side, t):
+        p, b = parts[t], bufs[t]
+        src = delta[t].at[rows_a[t], p.window(owner(1 - side, -s[t]))]
+        along_z(("a1", side, t), src, b["a1"].at[side], -s[t])
+
+    def merge_a(side, t):
+        b = bufs[t]
+        arrived("a2", side, t)
+        own_a[t, 0, side].wait()
+        add_up(b["merged_a"].at[side], b["own_a"].at[0, side], b["a2"].at[side])
+        along_z(("am", side, t), b["merged_a"].at[side], b["am"].at[side], s[t])
+
+    def raw_b(k, t):
+        p, b = parts[t], bufs[t]
+        src = delta[t].at[rows_b[t], p.window(owner(1, k * s[t]))]
+        along_y(("by", k, t), src, b["by"].at[k])
+
+    for t in both:
+        raw_a(0, t)
+    for t in both:
+        raw_b(2, t)
+    for t in both:
+        raw_a_alone(0, t)
+    for k in (3, 1):
+        for t in both:
+            raw_b(k, t)
 
     own_a, own_b, params = {}, {}, []
     for side in (0, 1):
@@ -122,46 +167,6 @@
         params.append(start_local(master[t], master_next[t]))
         params.append(start_local(moment[t], moment_next[t]))
 
-    plane = [(dy, dz) for dy in range(4) for dz in range(4)][1:]
-    across = [(dx, dc) for dx in range(4) for dc in range(2)][1:]
-    barrier = pltpu.get_barrier_semaphore()
-    for dy, dz in plane:
-        pl.semaphore_signal(barrier, inc=1, device_id=chip(dy=dy, dz=dz), device_id_type=MESH)
-    for dx, dc in across:
-        pl.semaphore_signal(barrier, inc=1, device_id=chip(dx=dx, dc=dc), device_id_type=MESH)
-    pl.semaphore_wait(barrier, len(plane) + len(across))
-
-    def raw_a(side, t):
-        p, b = parts[t], bufs[t]
-        src = delta[t].at[rows_a[t], p.window(owner(1 - side, 2))]
-        along_z(("a2", side, t), src, b["a2"].at[side], s[t])
-
-    def raw_a_alone(side, t):
-        p, b = parts[t], bufs[t]
-        src = delta[t].at[rows_a[t], p.window(owner(1 - side, -s[t]))]
-        along_z(("a1", side, t), src, b["a1"].at[side], -s[t])
-
-    def merge_a(side, t):
-        b = bufs[t]
-        arrived("a2", side, t)
-        own_a[t, 0, side].wait()
-        add_up(b["merged_a"].at[side], b["own_a"].at[0, side], b["a2"].at[side])
-        along_z(("am", side, t), b["merged_a"].at[side], b["am"].at[side], s[t])
-
-    def raw_b(k, t):
-        p, b = parts[t], bufs[t]
-        src = delta[t].at[rows_b[t], p.window(owner(1, k * s[t]))]
-        along_y(("by", k, t), src, b["by"].at[k])
-
-    for t in both:
-        raw_a(0, t)
-    for t in both:
-        raw_b(2, t)
-    for t in both:
-        raw_a_alone(0, t)
-    for k in (3, 1):
-        for t in both:
-            raw_b(k, t)
     for t in both:
         merge_a(0, t)
     for t in both:
@@ -207,6 +212,17 @@
             master_next[t][rows, :] = master_next[t][rows, :] - 0.567 * moment_next[t][rows, :]
 
         over_rows(parts[t].rows, base)
+
+    def early(name, t):
+        b = bufs[t]
+        for slot, dz in enumerate((s[t], -s[t])):
+            along_z((name, slot, t), b[name], b["got_" + name].at[slot], dz)
+        along_y((name, 2, t), b[name], b["got_" + name].at[2])
+
+    for t in both:
+        add_up(bufs[t]["u"], master_next[t])
+    for t in both:
+        early("u", t)
 
     line = jnp.zeros((1, 128), F32)
     for t in both:
@@ -229,6 +245,10 @@
     line1[pl.ds(0, 1)] = line
     for i, (dy, dz) in enumerate(plane):
         send(("n1", i), line1.at[pl.ds(0, 1)], line1.at[pl.ds(i + 1, 1)], chip(dy=dy, dz=dz))
+    for t in both:
+        add_up(bufs[t]["v"], bufs[t]["total"])
+    for t in both:
+        early("v", t)
     for i in range(len(plane)):
         arrived("n1", i)
     line2[pl.ds(0, 1)] = jnp.sum(line1[...], axis=0, keepdims=True)
@@ -239,54 +259,74 @@
     square_sum = jnp.sum(line2[...], axis=(0, 1), keepdims=True) * (1.0 / 64.0)
     factor = jnp.minimum(1.0, LIMIT / jnp.sqrt(square_sum + 1e-06)) * 0.125
 
-    def update(t, first, rows_here):
-        b = bufs[t]
-        scale = 1.33 * factor
+    scale = 1.33 * factor
+
+    def update(t, first, count, weights_too):
+        b = bufs[t]
         mine = parts[t].window(rep)
 
         def body(rows, _):
             rows = pl.ds(pl.multiple_of(first + rows.start, STEP), STEP)
             new = master_next[t][rows, :] - scale * b["total"][rows, :]
             master_next[t][rows, :] = new
-            weights[t][rows, mine] = new.astype(BF16)
-
-        over_rows(rows_here, body)
-
-    def out_at(t, rows, who):
-        return weights[t].at[rows, parts[t].window(who)]
+            if weights_too:
+                weights[t][rows, mine] = new.astype(BF16)
+
+        over_rows(count, body)
+
+    def next_moment(t):
+        b, m = bufs[t], moment_next[t]
+
+        def body(rows, _):
+            m[rows, :] = 0.9 * m[rows, :] + factor * b["total"][rows, :]
+
+        over_rows(parts[t].rows, body)
+
+    def work_out(t, u, v, who):
+        columns = parts[t].window(owner(*who))
+
+        def body(rows, _):
+            new = u[rows, :].astype(F32) - scale * v[rows, :].astype(F32)
+            weights[t][rows, columns] = new.astype(BF16)
+
+        over_rows(parts[t].g, body)
+
+    def work_out_got(t, slot, who):
+        arrived("u", slot, t)
+        arrived("v", slot, t)
+        work_out(t, bufs[t]["got_u"].at[slot], bufs[t]["got_v"].at[slot], who)
 
     def give(t, rows, dz, who):
-        key = ("w", t, rows is rows_a[t], dz, who)
-        place = out_at(t, rows, owner(*who))
+        place = weights[t].at[rows, parts[t].window(owner(*who))]
+        key = ("w", t, rows.start, rows.size, dz, who)
         if dz is None:
             along_y(key, place, place)
         else:
             along_z(key, place, place, dz)
 
     def got(t, rows, dz, who):
-        arrived("w", t, rows is rows_a[t], dz, who)
+        arrived("w", t, rows.start, rows.size, dz, who)
 
     own = (0, 0)
     for t in both:
-        update(t, 0, parts[t].a)
-        give(t, rows_a[t], None, own)
-    for t in both:
-        update(t, parts[t].a, parts[t].b)
+        update(t, parts[t].g, parts[t].a - parts[t].g, True)
+        give(t, rows_h[t], None, own)
+    for t in both:
+        update(t, parts[t].a, parts[t].b, True)
         for dz in (s[t], -s[t]):
             give(t, rows_b[t], dz, own)
     for t in both:
         give(t, rows_b[t], None, own)
     for t in both:
         for dz in (s[t], -s[t]):
-            give(t, rows_a[t], dz, own)
-
-    def next_moment(t):
-        b, m = bufs[t], moment_next[t]
-
-        def body(rows, _):
-            m[rows, :] = 0.9 * m[rows, :] + factor * b["total"][rows, :]
-
-        over_rows(parts[t].rows, body)
+            give(t, rows_h[t], dz, own)
+    for t in both:
+        work_out_got(t, 0, (0, -s[t]))
+        give(t, rows_g[t], s[t], (0, -s[t]))
+    for t in both:
+        work_out_got(t, 2, (1, 0))
+        for dz in (s[t], -s[t]):
+            give(t, rows_g[t], dz, (1, 0))
 
     for t in both:
         got(t, rows_b[t], s[t], own)
@@ -296,24 +336,31 @@
         got(t, rows_b[t], -s[t], own)
         give(t, rows_b[t], None, (0, s[t]))
     for t in both:
+        got(t, rows_h[t], None, own)
+        for dz in (s[t], -s[t]):
+            give(t, rows_h[t], dz, (1, 0))
+    for t in both:
+        got(t, rows_h[t], s[t], own)
+        give(t, rows_h[t], s[t], (0, -s[t]))
+    for t in both:
+        work_out(t, bufs[t]["u"], bufs[t]["v"], own)
+        work_out_got(t, 1, (0, s[t]))
+    for t in both:
+        update(t, 0, parts[t].g, False)
         next_moment(t)
-    for t in both:
-        got(t, rows_a[t], None, own)
-        for dz in (s[t], -s[t]):
-            give(t, rows_a[t], dz, (1, 0))
     for t in both:
         got(t, rows_b[t], s[t], (0, -s[t]))
         give(t, rows_b[t], None, (0, 2))
     for t in both:
-        got(t, rows_a[t], s[t], own)
-        give(t, rows_a[t], s[t], (0, -s[t]))
-    for t in both:
-        got(t, rows_a[t], s[t], (1, 0))
+        got(t, rows_g[t], s[t], (1, 0))
+        got(t, rows_h[t], s[t], (1, 0))
         give(t, rows_a[t], s[t], (1, -s[t]))
     for t in both:
-        got(t, rows_a[t], -s[t], own)
-        got(t, rows_a[t], -s[t], (1, 0))
-        got(t, rows_a[t], s[t], (0, -s[t]))
+        got(t, rows_h[t], -s[t], own)
+        got(t, rows_g[t], -s[t], (1, 0))
+        got(t, rows_h[t], -s[t], (1, 0))
+        got(t, rows_g[t], s[t], (0, -s[t]))
+        got(t, rows_h[t], s[t], (0, -s[t]))
         got(t, rows_a[t], s[t], (1, -s[t]))
         for who in (own, (0, -s[t]), (0, s[t]), (0, 2)):
             got(t, rows_b[t], None, who)
@@ -322,7 +369,7 @@
 
 
 def shapes(p):
-    a, b, c = p.a, p.b, p.columns
+    a, b, g, c = p.a, p.b, p.g, p.columns
     return {
         "own_a": (2, 2, a, c),
         "own_b": (4, b, c),
@@ -337,6 +384,10 @@
         "b1": (b, c),
         "bm": (b, c),
         "sum_b": (3, b, c),
+        "u": (g, c),
+        "v": (g, c),
+        "got_u": (3, g, c),
+        "got_v": (3, g, c),
         "total": (p.rows, c),
     }
 
@@ -370,8 +421,8 @@
             *scratch(parts[1]),
             pltpu.VMEM((16, 128), F32),
             pltpu.VMEM((8, 128), F32),
-            pltpu.SemaphoreType.DMA((80,)),
-            pltpu.SemaphoreType.DMA((80,)),
+            pltpu.SemaphoreType.DMA((104,)),
+            pltpu.SemaphoreType.DMA((104,)),
             pltpu.SemaphoreType.DMA((32,)),
         ],
         compiler_params=pltpu.CompilerParams(

time: 134 us -> 131 us (0.978)
  Pallas kernels: 133 us -> 130 us
    pallas_call x1, Pallas kernels: 128 us -> 126 us  [on_device(): pl.pallas_call(functools.partial(kernel, parts), out_shape=[pltpu.VMEM(*o...]
where the time goes in v3:
time: 131 us
  Pallas kernels  130 us (99%)
    pallas_call x1, Pallas kernels, on_device(): pl.pallas_call(functools.partial(kernel, parts), out_shape=[pltpu.VMEM(*o...  126 us
    pallas_call x1, Pallas kernels, on_device(): pl.pallas_call(write_out, out_shape=[jax.ShapeDtypeStruct(*out) for out i...  4.61 us

profile of v3, /device:TPU:1, one launch (start us, length us, event | category | flops | bytes accessed | tf_op | source)
XLA Modules:
  0.0 131.1 jit_solution(15906263998309328406)
XLA Ops:
  0.6 125.9 %outer_step.1 = (bf16[512,4096]{1,0:T(8,128)(2,1)S(1)}, bf16[256,8192]{1,0:T(8,128)(2,1)S(1)}, f32[512,512]{1,0:T(8,128)S(1)}, f32[256,1024]{1,0:T(8,128)S(1)}, ...) custom-call(bf16[512,4096]{1,0:T(8,128)(2,1)} %bitcast.2, bf16[256,8192]{1,0:T(8,128)(2,1)} %bitcast.3, ...), custom_call_target="tpu_custom_call" | custom-call | tf_op jit(solution)/shard_map/outer_step/pallas_call | solution.py:414
  126.5 4.6 %write_out.1 = (bf16[512,4096]{1,0:T(8,128)(2,1)}, bf16[256,8192]{1,0:T(8,128)(2,1)}, f32[512,512]{1,0:T(8,128)}, f32[256,1024]{1,0:T(8,128)}, f32[512,512]{1,0:T(8,128)}, /*index=5*/f32[256,1024]{1,0:T(8,128)}) custom-call(bf16[512,4096]{1,0:T(8,128)(2,1)S(1)} %get-tuple-element.12.refs_0_, bf16[256,8192]{1,0:T(8,128)(2,1)S(1)} %get-tuple-element.13.refs_1_, ...), custom_call_target="tpu_custom_call" | custom-call | tf_op jit(solution)/shard_map/write_out/pallas_call | solution.py:433

commit v4 on v3

--- a/solution.py
+++ b/solution.py
@@ -67,7 +67,7 @@
         names = list(shapes(p))
         bufs.append(dict(zip(names, refs[at : at + len(names)])))
         at += len(names)
-    line1, line2, send_sem, recv_sem, local_sem = refs[at:]
+    line1, line2, links, send_sem, recv_sem, local_sem = refs[at:]
 
     rep, shard = lax.axis_index("rep"), lax.axis_index("fsdp")
     y_hi, z = rep // 4, lax.rem(rep, 4)
@@ -112,14 +112,19 @@
     rows_h = [pl.ds(p.g, p.a - p.g) for p in parts]
     s = [p.sign for p in parts]
 
-    plane = [(dy, dz) for dy in range(4) for dz in range(4)][1:]
-    across = [(dx, dc) for dx in range(4) for dc in range(2)][1:]
+    around = {"x": (chip(dx=1), chip(dx=3)), "y": (chip(dy=1), chip(dy=3)), "z": (chip(dz=1), chip(dz=3))}
+    near = [*around["z"], chip(dy=2), chip(dc=1), *around["y"], *around["x"]]
     barrier = pltpu.get_barrier_semaphore()
-    for dy, dz in plane:
-        pl.semaphore_signal(barrier, inc=1, device_id=chip(dy=dy, dz=dz), device_id_type=MESH)
-    for dx, dc in across:
-        pl.semaphore_signal(barrier, inc=1, device_id=chip(dx=dx, dc=dc), device_id_type=MESH)
-    pl.semaphore_wait(barrier, len(plane) + len(across))
+    for target in near:
+        pl.semaphore_signal(barrier, inc=1, device_id=target, device_id_type=MESH)
+    pl.semaphore_wait(barrier, len(near))
+
+    def tell(i):
+        for target in around["xyyzz"[i]]:
+            pl.semaphore_signal(links.at[i], inc=1, device_id=target, device_id_type=MESH)
+
+    def told(i):
+        pl.semaphore_wait(links.at[i], 2)
 
     def raw_a(side, t):
         p, b = parts[t], bufs[t]
@@ -167,8 +172,11 @@
         params.append(start_local(master[t], master_next[t]))
         params.append(start_local(moment[t], moment_next[t]))
 
+    tell(0)
     for t in both:
         merge_a(0, t)
+    told(0)
+    tell(1)
     for t in both:
         raw_a(1, t)
     for t in both:
@@ -179,12 +187,16 @@
         own_b[t, 2].wait()
         add_up(b["sum_b"].at[0], b["own_b"].at[2], b["by"].at[2])
         along_z(("b2", t), b["sum_b"].at[0], b["b2"], s[t])
+    told(1)
+    tell(2)
     for t in both:
         b = bufs[t]
         arrived("by", 3, t)
         own_b[t, 3].wait()
         add_up(b["sum_b"].at[1], b["own_b"].at[3], b["by"].at[3])
         along_z(("b1", t), b["sum_b"].at[1], b["b1"], -s[t])
+    told(2)
+    tell(3)
     for t in both:
         b = bufs[t]
         arrived("a1", 0, t)
@@ -194,8 +206,11 @@
         along_y(("ay", t), b["sum_a"], b["ay"])
     for t in both:
         raw_b(0, t)
+    told(3)
+    tell(4)
     for t in both:
         merge_a(1, t)
+    told(4)
     for t in both:
         b = bufs[t]
         arrived("by", 1, t)
@@ -242,21 +257,21 @@
         terms = (b["own_b"].at[0], b["by"].at[0], b["b1"], b["bm"])
         line += add_up_squares(b["total"].at[rows_b[t]], *terms)
 
-    line1[pl.ds(0, 1)] = line
-    for i, (dy, dz) in enumerate(plane):
-        send(("n1", i), line1.at[pl.ds(0, 1)], line1.at[pl.ds(i + 1, 1)], chip(dy=dy, dz=dz))
+    line1[core] = line
+    send(("n1",), line1.at[core], line1.at[core], chip(dc=1))
+    arrived("n1")
+    here = (x * 4 + y_hi * 2 + y_lo) * 4 + z
+    line2[here] = jnp.sum(line1[...], axis=0)
+    others = [(dx, dy, dz) for dx in range(4) for dy in range(4) for dz in range(4)][1:]
+    for dx, dy, dz in others:
+        send(("n2", dx, dy, dz), line2.at[here], line2.at[here], chip(dx=dx, dy=dy, dz=dz))
     for t in both:
         add_up(bufs[t]["v"], bufs[t]["total"])
     for t in both:
         early("v", t)
-    for i in range(len(plane)):
-        arrived("n1", i)
-    line2[pl.ds(0, 1)] = jnp.sum(line1[...], axis=0, keepdims=True)
-    for i, (dx, dc) in enumerate(across):
-        send(("n2", i), line2.at[pl.ds(0, 1)], line2.at[pl.ds(i + 1, 1)], chip(dx=dx, dc=dc))
-    for i in range(len(across)):
-        arrived("n2", i)
-    square_sum = jnp.sum(line2[...], axis=(0, 1), keepdims=True) * (1.0 / 64.0)
+    for there in others:
+        arrived("n2", *there)
+    square_sum = jnp.sum(jnp.sum(line2[...], axis=0), axis=1, keepdims=True) * (1.0 / 64.0)
     factor = jnp.minimum(1.0, LIMIT / jnp.sqrt(square_sum + 1e-06)) * 0.125
 
     scale = 1.33 * factor
@@ -419,10 +434,11 @@
         scratch_shapes=[
             *scratch(parts[0]),
             *scratch(parts[1]),
-            pltpu.VMEM((16, 128), F32),
-            pltpu.VMEM((8, 128), F32),
-            pltpu.SemaphoreType.DMA((104,)),
-            pltpu.SemaphoreType.DMA((104,)),
+            pltpu.VMEM((2, 1, 128), F32),
+            pltpu.VMEM((64, 1, 128), F32),
+            pltpu.SemaphoreType.REGULAR((5,)),
+            pltpu.SemaphoreType.DMA((144,)),
+            pltpu.SemaphoreType.DMA((144,)),
             pltpu.SemaphoreType.DMA((32,)),
         ],
         compiler_params=pltpu.CompilerParams(

time: 131 us -> 130 us (level)
    pallas_call x1, Pallas kernels: 126 us -> 124 us  [on_device(): pl.pallas_call(functools.partial(kernel, parts), out_shape=[pltpu.VMEM(*o...]
where the time goes in v4:
time: 130 us
  Pallas kernels  129 us (99%)
    pallas_call x1, Pallas kernels, on_device(): pl.pallas_call(functools.partial(kernel, parts), out_shape=[pltpu.VMEM(*o...  124 us
    pallas_call x1, Pallas kernels, on_device(): pl.pallas_call(write_out, out_shape=[jax.ShapeDtypeStruct(*out) for out i...  4.61 us

profile of v4, /device:TPU:1, one launch (start us, length us, event | category | flops | bytes accessed | tf_op | source)
XLA Modules:
  0.0 129.5 jit_solution(13711050084956411838)
XLA Ops:
  0.6 124.3 %outer_step.1 = (bf16[512,4096]{1,0:T(8,128)(2,1)S(1)}, bf16[256,8192]{1,0:T(8,128)(2,1)S(1)}, f32[512,512]{1,0:T(8,128)S(1)}, f32[256,1024]{1,0:T(8,128)S(1)}, ...) custom-call(bf16[512,4096]{1,0:T(8,128)(2,1)} %bitcast.2, bf16[256,8192]{1,0:T(8,128)(2,1)} %bitcast.3, ...), custom_call_target="tpu_custom_call" | custom-call | tf_op jit(solution)/shard_map/outer_step/pallas_call | solution.py:429
  124.9 4.6 %write_out.1 = (bf16[512,4096]{1,0:T(8,128)(2,1)}, bf16[256,8192]{1,0:T(8,128)(2,1)}, f32[512,512]{1,0:T(8,128)}, f32[256,1024]{1,0:T(8,128)}, f32[512,512]{1,0:T(8,128)}, /*index=5*/f32[256,1024]{1,0:T(8,128)}) custom-call(bf16[512,4096]{1,0:T(8,128)(2,1)S(1)} %get-tuple-element.12.refs_0_, bf16[256,8192]{1,0:T(8,128)(2,1)S(1)} %get-tuple-element.13.refs_1_, ...), custom_call_target="tpu_custom_call" | custom-call | tf_op jit(solution)/shard_map/write_out/pallas_call | solution.py:449

commit v5 on v4

--- a/solution.py
+++ b/solution.py
@@ -12,7 +12,7 @@
 BF16, F32 = jnp.bfloat16, jnp.float32
 LIMIT = 0.25 * math.sqrt(2.0 * 8192 * 4096)
 FIRST_Z = 9 / 16
-EARLY = 3 / 16
+EARLY = 1 / 4
 STEP = 16
 
 

time: 130 us -> 129 us (level)
  no operation moved by 1% of the time
where the time goes in v5:
time: 129 us; the launch traced here: 128 us
  Pallas kernels  128 us (99%)
    pallas_call x1, Pallas kernels, on_device(): pl.pallas_call(functools.partial(kernel, parts), out_shape=[pltpu.VMEM(*o...  123 us
    pallas_call x1, Pallas kernels, on_device(): pl.pallas_call(write_out, out_shape=[jax.ShapeDtypeStruct(*out) for out i...  4.61 us

profile of v5, /device:TPU:1, one launch (start us, length us, event | category | flops | bytes accessed | tf_op | source)
XLA Modules:
  0.0 128.4 jit_solution(15251010710409473021)
XLA Ops:
  0.6 123.2 %outer_step.1 = (bf16[512,4096]{1,0:T(8,128)(2,1)S(1)}, bf16[256,8192]{1,0:T(8,128)(2,1)S(1)}, f32[512,512]{1,0:T(8,128)S(1)}, f32[256,1024]{1,0:T(8,128)S(1)}, ...) custom-call(bf16[512,4096]{1,0:T(8,128)(2,1)} %bitcast.2, bf16[256,8192]{1,0:T(8,128)(2,1)} %bitcast.3, ...), custom_call_target="tpu_custom_call" | custom-call | tf_op jit(solution)/shard_map/outer_step/pallas_call | solution.py:429
  123.8 4.6 %write_out.1 = (bf16[512,4096]{1,0:T(8,128)(2,1)}, bf16[256,8192]{1,0:T(8,128)(2,1)}, f32[512,512]{1,0:T(8,128)}, f32[256,1024]{1,0:T(8,128)}, f32[512,512]{1,0:T(8,128)}, /*index=5*/f32[256,1024]{1,0:T(8,128)}) custom-call(bf16[512,4096]{1,0:T(8,128)(2,1)S(1)} %get-tuple-element.12.refs_0_, bf16[256,8192]{1,0:T(8,128)(2,1)S(1)} %get-tuple-element.13.refs_1_, ...), custom_call_target="tpu_custom_call" | custom-call | tf_op jit(solution)/shard_map/write_out/pallas_call | solution.py:449

commit v6 on v5

--- a/solution.py
+++ b/solution.py
@@ -259,16 +259,17 @@
 
     line1[core] = line
     send(("n1",), line1.at[core], line1.at[core], chip(dc=1))
+    for t in both:
+        add_up(bufs[t]["v"], bufs[t]["total"])
     arrived("n1")
     here = (x * 4 + y_hi * 2 + y_lo) * 4 + z
     line2[here] = jnp.sum(line1[...], axis=0)
     others = [(dx, dy, dz) for dx in range(4) for dy in range(4) for dz in range(4)][1:]
-    for dx, dy, dz in others:
+    for k, (dx, dy, dz) in enumerate(others):
+        if k == 15:
+            for t in both:
+                early("v", t)
         send(("n2", dx, dy, dz), line2.at[here], line2.at[here], chip(dx=dx, dy=dy, dz=dz))
-    for t in both:
-        add_up(bufs[t]["v"], bufs[t]["total"])
-    for t in both:
-        early("v", t)
     for there in others:
         arrived("n2", *there)
     square_sum = jnp.sum(jnp.sum(line2[...], axis=0), axis=1, keepdims=True) * (1.0 / 64.0)

time: 129 us -> 128 us (level)
  no operation moved by 1% of the time
where the time goes in v6:
time: 128 us
  Pallas kernels  128 us (100%)
    pallas_call x1, Pallas kernels, on_device(): pl.pallas_call(functools.partial(kernel, parts), out_shape=[pltpu.VMEM(*o...  123 us
    pallas_call x1, Pallas kernels, on_device(): pl.pallas_call(write_out, out_shape=[jax.ShapeDtypeStruct(*out) for out i...  4.61 us

profile of v6, /device:TPU:1, one launch (start us, length us, event | category | flops | bytes accessed | tf_op | source)
XLA Modules:
  0.0 128.4 jit_solution(13981107245675269304)
XLA Ops:
  0.6 123.1 %outer_step.1 = (bf16[512,4096]{1,0:T(8,128)(2,1)S(1)}, bf16[256,8192]{1,0:T(8,128)(2,1)S(1)}, f32[512,512]{1,0:T(8,128)S(1)}, f32[256,1024]{1,0:T(8,128)S(1)}, ...) custom-call(bf16[512,4096]{1,0:T(8,128)(2,1)} %bitcast.2, bf16[256,8192]{1,0:T(8,128)(2,1)} %bitcast.3, ...), custom_call_target="tpu_custom_call" | custom-call | tf_op jit(solution)/shard_map/outer_step/pallas_call | solution.py:430
  123.8 4.6 %write_out.1 = (bf16[512,4096]{1,0:T(8,128)(2,1)}, bf16[256,8192]{1,0:T(8,128)(2,1)}, f32[512,512]{1,0:T(8,128)}, f32[256,1024]{1,0:T(8,128)}, f32[512,512]{1,0:T(8,128)}, /*index=5*/f32[256,1024]{1,0:T(8,128)}) custom-call(bf16[512,4096]{1,0:T(8,128)(2,1)S(1)} %get-tuple-element.12.refs_0_, bf16[256,8192]{1,0:T(8,128)(2,1)S(1)} %get-tuple-element.13.refs_1_, ...), custom_call_target="tpu_custom_call" | custom-call | tf_op jit(solution)/shard_map/write_out/pallas_call | solution.py:450
